TPU v7x, 128 devices: a whole 4x4x4 slice. The times are simulated.
128 devices in a mesh: seq: 32 (over y, z, core), head: 4 (over x).
Axes of the slice: x: 4, y: 4, z: 4, core: 2. Of those that a mesh axis runs over, the one named last changes fastest.
Arguments:
- image_patches: bfloat16 [32, 256, 1152], P('seq', None, 'head'), may hold values from -6 to 6
- text_embed: bfloat16 [8192, 2048], P('seq', 'head'), may hold values from -6 to 6
- image_start: int32 [32], replicated, may hold values from 0 to 126, as said below
- image_forget: float32 [32], replicated, may hold values from 0.001 to 0.3
- adapter: bfloat16 [1152, 2048], P('head'), may hold values from -0.1875 to 0.1875
- norm_gain: float32 [2048], replicated, may hold values from 0.5 to 1.5
- in_proj: bfloat16 [2048, 4, 2048], P(None, None, 'head'), may hold values from -0.125 to 0.125
- decay_proj: bfloat16 [2048, 16], P(None, 'head'), may hold values from -0.125 to 0.125
- head_decay_ceiling: float32 [16], P('head'), may hold values from 0 to 1, as said below
- out_gain: float32 [16, 128], P('head'), may hold values from 0.5 to 1.5
- out_proj: bfloat16 [2048, 2048], P('head'), may hold values from -0.125 to 0.125
Outputs:
- image_out: bfloat16 [32, 256, 2048], P('seq', None, 'head')
- text_out: bfloat16 [8192, 2048], P('seq', 'head')
Inputs may be any that keep to these rules, and one draw needn't show every extreme that they name: `image_start`: each entry is even; the images take distinct pairs of blocks. The merged piece of 512 tokens on one device of seq never holds both the image and the text that one device of seq holds in the source layout. `head_decay_ceiling`: Positive.
All inputs are finite; a program needn't handle non-finite values.
Results may differ from a plain program's by a relative error of at most 0.0095.
Values may be sent and summed in bfloat16 or wider, within the bound.
No kernel may reach another device: no remote copies, remote signals or barrier semaphores. Data moves between devices by JAX's collectives and lax.ppermute only.
A program may use at most 128 MiB of HBM per device.

v0:
```python
import jax
import jax.numpy as jnp
from jax import lax
from jax.sharding import Mesh
from jax.sharding import PartitionSpec as P

SEQ = ("seq_0", "seq_1", "seq_2")
EPSILON = 1e-06


def split_up(array, dim, length):
    shape = array.shape
    pieces = array.reshape(*shape[:dim], length, shape[dim] // length, *shape[dim + 1 :])
    return jnp.moveaxis(pieces, dim, 0)


def sent_and_summed(array, axis, dim):
    pieces = split_up(array, dim, lax.axis_size(axis))
    arrived = lax.all_to_all(pieces, axis, split_axis=0, concat_axis=0, tiled=True)
    return arrived.sum(axis=0)


def in_order(pieces, dim):
    shape = list(pieces.shape[1:])
    shape[dim] *= pieces.shape[0]
    return jnp.moveaxis(pieces, 0, dim).reshape(shape)


def copy_for_each(array, axis):
    length = lax.axis_size(axis)
    return lax.all_to_all(
        jnp.broadcast_to(array[None], (length, *array.shape)), axis, 0, 0, tiled=True
    )


def gathered_copies(array, axis, dim):
    return in_order(copy_for_each(array, axis), dim)


def neutral_like(array, identity):
    return jax.tree.map(
        lambda a, e: jnp.broadcast_to(jnp.asarray(e, a.dtype), a.shape), array, identity
    )


def entering_2(array, axes, combine, identity):
    before = start = neutral_like(array, identity)
    total = array
    for axis in reversed(axes):
        length, position = (lax.axis_size(axis), lax.axis_index(axis))
        pieces = jax.tree.map(
            lambda part, kind: lax.all_gather(part.astype(kind), axis),
            total,
            (jnp.bfloat16, jnp.bfloat16),
        )
        inside, total = (start, start)
        for k in range(length):
            passed = k < position
            total = combine(
                total, jax.tree.map(lambda part, own: part[k].astype(own.dtype), pieces, array)
            )
            inside = jax.tree.map(lambda new, old: jnp.where(passed, new, old), total, inside)
        before = combine(inside, before)
    return before


def sent_and_summed_2(array, axis, dim):
    pieces = split_up(array, dim, lax.axis_size(axis))
    arrived = lax.all_to_all(pieces, axis, split_axis=0, concat_axis=0, tiled=True)
    return arrived.astype(jnp.float32).sum(axis=0)


def rms_scale(values, gain_row):
    mean_square = jnp.mean(values * values, axis=-1, keepdims=True)
    return values * lax.rsqrt(mean_square + EPSILON) * gain_row


def shards(
    image_patches,
    text_embed,
    image_start,
    image_forget,
    adapter,
    norm_gain,
    in_proj,
    decay_proj,
    head_decay_ceiling,
    out_gain,
    out_proj,
):
    seq_count = lax.axis_size(SEQ)
    my_index = lax.axis_index(SEQ)
    patch_row_block = text_embed.shape[0]
    local_width = text_embed.shape[1]
    share_rows = patch_row_block // seq_count
    unit_count = 2 * seq_count
    token_rows = 2 * patch_row_block
    unit_ids = jnp.arange(unit_count, dtype=jnp.int32)
    device_ids = jnp.arange(seq_count, dtype=jnp.int32)
    unit_of_image = image_start // 2
    image_hits = (unit_of_image[:, None] == unit_ids[None, :]).astype(jnp.int32)
    is_image = jnp.sum(image_hits, axis=0)
    image_here = jnp.sum(image_hits * device_ids[:, None], axis=0)
    is_text = 1 - is_image
    text_here = jnp.cumsum(is_text) - is_text
    text_pick = ((is_text[None, :] == 1) & (text_here[None, :] == device_ids[:, None])).astype(
        jnp.int32
    )
    text_unit = jnp.sum(text_pick * unit_ids[None, :], axis=1)
    source = jnp.where(is_image == 1, image_here, text_here)
    my_units = 2 * my_index + jnp.arange(2, dtype=jnp.int32)
    unit_image = jnp.take(is_image, my_units)
    partial_value = jnp.dot(image_patches[0], adapter, preferred_element_type=jnp.float32)
    embedded = sent_and_summed(partial_value, "head", 1).astype(jnp.bfloat16)
    units_here = jnp.stack([embedded, text_embed]).reshape(2, seq_count, share_rows, local_width)
    spread = lax.all_to_all(units_here, SEQ, split_axis=1, concat_axis=1, tiled=True)
    table = spread.reshape(unit_count, share_rows, local_width)
    pick_index = is_text * seq_count + source
    outgoing_units = jnp.take(table, pick_index, axis=0).reshape(
        seq_count, 2, share_rows, local_width
    )
    arrived = lax.all_to_all(outgoing_units, SEQ, split_axis=0, concat_axis=2, tiled=True)
    merged = arrived.reshape(token_rows, local_width)
    full_rows = gathered_copies(merged, "head", 1)
    normed = rms_scale(full_rows.astype(jnp.float32), norm_gain).astype(jnp.bfloat16)
    model_width = in_proj.shape[0]
    head_count = head_decay_ceiling.shape[0]
    head_width = out_gain.shape[1]
    projected = jnp.dot(
        normed, in_proj.reshape(model_width, -1), preferred_element_type=jnp.float32
    )
    projected = projected.astype(jnp.bfloat16).reshape(token_rows, 4, head_count, head_width)
    gate_preactivation = jnp.dot(normed, decay_proj, preferred_element_type=jnp.float32)
    forget_element = jnp.where(
        unit_image == 1, jnp.log1p(-jnp.take(image_forget, jnp.take(image_here, my_units))), 0.0
    )
    start_offsets = jnp.arange(token_rows, dtype=jnp.int32) % patch_row_block == 0
    surge_logarithm = jnp.where(start_offsets, jnp.repeat(forget_element, patch_row_block), 0.0)
    decay_logarithm = (
        -head_decay_ceiling[None, :] * jax.nn.sigmoid(gate_preactivation) + surge_logarithm[:, None]
    )
    queries = projected[:, 0]
    key_rows = projected[:, 1]
    value_rows = projected[:, 2]
    gate_rows = projected[:, 3]
    within = jnp.cumsum(decay_logarithm, axis=0)
    span_decay = within[-1]
    scores = jnp.einsum("thd,shd->hts", queries, key_rows, preferred_element_type=jnp.float32)
    lagged = within.T[:, :, None] - within.T[:, None, :]
    row_ids = jnp.arange(token_rows, dtype=jnp.int32)
    causal = (row_ids[:, None] >= row_ids[None, :])[None]
    weights = jnp.where(causal, scores * jnp.exp(jnp.where(causal, lagged, 0.0)), 0.0).astype(
        jnp.bfloat16
    )
    inner_part = jnp.einsum("hts,shd->thd", weights, value_rows, preferred_element_type=jnp.float32)
    weighted_keys = key_rows.astype(jnp.float32) * jnp.exp(span_decay[None, :] - within)[:, :, None]
    local_state = jnp.einsum("thd,the->hde", weighted_keys, value_rows.astype(jnp.float32))

    def combine(earlier, later_part):
        return (
            earlier[0] + later_part[0],
            jnp.exp(later_part[0])[:, None, None] * earlier[1] + later_part[1],
        )

    identity = (jnp.zeros_like(span_decay), jnp.zeros_like(local_state))
    decay_before, entering = entering_2((span_decay, local_state), SEQ, combine, identity)
    carried = jnp.exp(within)[:, :, None] * jnp.einsum(
        "thd,hde->the", queries.astype(jnp.float32), entering
    )
    attended = inner_part + carried
    gated = rms_scale(attended, out_gain) * jax.nn.silu(gate_rows.astype(jnp.float32))
    gated = gated.astype(jnp.bfloat16).reshape(token_rows, -1)
    partial_out = jnp.dot(gated, out_proj, preferred_element_type=jnp.float32)
    summed = sent_and_summed_2(partial_out.astype(jnp.bfloat16), "head", 1)
    result = (merged.astype(jnp.float32) + summed).astype(jnp.bfloat16)
    result_shares = result.reshape(2, seq_count, share_rows, local_width)
    back_spread = lax.all_to_all(result_shares, SEQ, split_axis=1, concat_axis=1, tiled=True)
    back_table = back_spread.reshape(unit_count, share_rows, local_width)
    wanted = jnp.stack([unit_of_image, text_unit], axis=1).reshape(-1)
    back_index = wanted % 2 * seq_count + wanted // 2
    outgoing = jnp.take(back_table, back_index, axis=0).reshape(
        seq_count, 2, share_rows, local_width
    )
    returned = lax.all_to_all(outgoing, SEQ, split_axis=0, concat_axis=2, tiled=True)
    image_out = returned[:, 0]
    text_out = returned[0, 1]
    return (image_out, text_out)


def solution(mesh):
    split = Mesh(
        mesh.devices.reshape(4, 4, 2, mesh.shape["head"]), ("seq_0", "seq_1", "seq_2", "head")
    )
    return jax.shard_map(
        shards,
        mesh=split,
        in_specs=(
            P(SEQ, None, "head"),
            P(SEQ, "head"),
            P(),
            P(),
            P("head", None),
            P(),
            P(None, None, "head"),
            P(None, "head"),
            P("head"),
            P("head", None),
            P("head", None),
        ),
        out_specs=(P(SEQ, None, "head"), P(SEQ, "head")),
        check_vma=False,
    )
```

profile of v0, /device:TPU:1, one launch (start us, length us, event | category | flops | bytes accessed | tf_op | source)
XLA Modules:
  0.0 257.9 jit_solution(2699861484524103100)
XLA Ops:
  0.6 3.5 %convolution_bitcast_fusion = f32[4,256,512]{2,1,0:T(8,128)} fusion(bf16[36,4,8,512]{3,2,1,0:T(8,128)(2,1)} %bitcast.304, bf16[1,256,288]{1,2,0:T(8,128)(2,1)} %param.15), kind=kOutput, calls=%fused_computation.15 | convolution fusion | flops 301989888 | bytes 3424256 | tf_op jit(solution)/shard_map/dot_general | solution.py:113
  4.2 5.0 %all-to-all-start = ((f32[4,256,512]{2,1,0:T(8,128)}), f32[4,256,512]{2,1,0:T(8,128)}, u32[]{:S(2)}, u32[]{:S(2)}) async-start(f32[4,256,512]{2,1,0:T(8,128)} %convolution_bitcast_fusion), calls=%async_computation | async-start | bytes 4194304 | tf_op jit(solution)/shard_map/all_to_all | solution.py:19
  9.2 25.9 %all-to-all-done = f32[4,256,512]{2,1,0:T(8,128)} async-done(((f32[4,256,512]{2,1,0:T(8,128)}), f32[4,256,512]{2,1,0:T(8,128)}, u32[]{:S(2)}, u32[]{:S(2)}) %all-to-all-start) | async-done | bytes 2097184 | tf_op jit(solution)/shard_map/all_to_all | solution.py:19
  35.1 1.8 reduce_sum.65
  37.8 9.9 %all-to-all-start.1 = ((bf16[2,32,8,512]{3,2,0,1:T(8,128)(2,1)}), bf16[2,32,8,512]{3,2,0,1:T(8,128)(2,1)S(1)}, u32[]{:S(2)}, u32[]{:S(2)}) async-start(bf16[2,32,8,512]{3,2,0,1:T(8,128)(2,1)} %pad_maximum_fusion), calls=%async_computation.1 | async-start | bytes 1048576 | tf_op jit(solution)/shard_map/all_to_all | solution.py:116
  48.1 11.2 %all-to-all-done.1 = bf16[2,32,8,512]{3,2,0,1:T(8,128)(2,1)S(1)} async-done(((bf16[2,32,8,512]{3,2,0,1:T(8,128)(2,1)}), bf16[2,32,8,512]{3,2,0,1:T(8,128)(2,1)S(1)}, u32[]{:S(2)}, u32[]{:S(2)}) %all-to-all-start.1) | async-done | bytes 524320 | tf_op jit(solution)/shard_map/all_to_all | solution.py:116
  60.1 15.0 %all_to_all.58 = bf16[32,2,8,512]{3,2,1,0:T(8,128)(2,1)S(1)} all-to-all(bf16[32,2,8,512]{3,2,1,0:T(8,128)(2,1)S(1)} %bitcast.299), channel_id=1, replica_groups=mesh['seq_0'=4,'seq_1'=4,'seq_2'=2,'head'=4] {'seq_0','seq_1','seq_2'}, dimensions={0} | all-to-all | bytes 1048576 | tf_op jit(solution)/shard_map/all_to_all | solution.py:122
  78.7 4.8 %all-to-all-start.3 = ((bf16[4,512,512]{1,2,0:T(8,128)(2,1)}), bf16[4,512,512]{1,2,0:T(8,128)(2,1)}, u32[]{:S(2)}, u32[]{:S(2)}) async-start(bf16[4,512,512]{1,2,0:T(8,128)(2,1)} %broadcast_in_dim.53), calls=%async_computation.3 | async-start | bytes 4194304 | tf_op jit(solution)/shard_map/all_to_all | solution.py:31
  85.6 10.2 %copy.158 = bf16[256,8,4,512]{3,1,2,0:T(8,128)(2,1)} copy(bf16[256,8,4,512]{3,2,1,0:T(4,128)(2,1)} %bitcast.292) | data formatting | bytes 16777216
  96.6 13.5 %all-to-all-done.3 = bf16[4,512,512]{1,2,0:T(8,128)(2,1)} async-done(((bf16[4,512,512]{1,2,0:T(8,128)(2,1)}), bf16[4,512,512]{1,2,0:T(8,128)(2,1)}, u32[]{:S(2)}, u32[]{:S(2)}) %all-to-all-start.3) | async-done | bytes 2097184 | tf_op jit(solution)/shard_map/all_to_all | solution.py:31
  110.1 2.1 multiply_reduce_fusion
  112.2 2.1 fusion.1
  116.8 2.2 multiply_convert_fusion
  119.0 9.1 %convolution_convert_fusion.1 = bf16[512,2048]{1,0:T(8,128)(2,1)} fusion(bf16[512,2048]{0,1:T(8,128)(2,1)S(1)} %bitcast.303, bf16[2048,2048]{1,0:T(8,128)(2,1)} %bitcast.293), kind=kOutput, calls=%fused_computation.13 | convolution fusion | flops 4296015872 | bytes 12582912 | tf_op jit(solution)/shard_map/dot_general | solution.py:129
  128.1 4.4 %reshape.369 = bf16[512,4,4,128]{3,2,1,0:T(4,128)(2,1)} reshape(bf16[512,2048]{1,0:T(8,128)(2,1)} %convolution_convert_fusion.1) | data formatting | bytes 4194304 | tf_op jit(solution)/shard_map/reshape | solution.py:132
  132.6 3.2 %fusion.128 = (bf16[512,1,4,128]{3,2,1,0:T(4,128)(2,1)}, bf16[512,1,4,128]{3,2,1,0:T(4,128)(2,1)}, bf16[512,1,4,128]{3,2,1,0:T(4,128)(2,1)S(1)}, bf16[512,1,4,128]{3,2,1,0:T(4,128)(2,1)}) fusion(bf16[512,4,4,128]{3,2,1,0:T(4,128)(2,1)} %reshape.369), kind=kLoop, calls=%fused_computation.240 | loop fusion | bytes 4194304 | tf_op jit(solution)/shard_map/slice | solution.py:145
  136.9 1.9 convolution_convert_fusion.2
  138.8 2.2 all-gather
  141.0 1.8 all-gather.1
  143.0 9.9 %all_gather.31 = bf16[4,4,128,128]{3,2,1,0:T(8,128)(2,1)S(1)} all-gather(bf16[1,4,128,128]{3,2,1,0:T(8,128)(2,1)S(1)} %fusion.52), channel_id=1, replica_groups=mesh['seq_0'=4,'seq_1'=4,'seq_2'=2,'head'=4] {'seq_1'}, dimensions={0}, use_global_device_ids=true | all-gather | bytes 655360 | tf_op jit(solution)/shard_map/all_gather | solution.py:52
  152.9 6.5 %all-gather.2 = bf16[4,1,4]{2,1,0:T(2,128)(2,1)S(1)} all-gather(bf16[1,1,4]{2,1,0:T(2,128)(2,1)S(1)} %get-tuple-element.32), channel_id=1, replica_groups=mesh['seq_0'=4,'seq_1'=4,'seq_2'=2,'head'=4] {'seq_1'}, dimensions={0}, use_global_device_ids=true | all-gather | bytes 40 | tf_op jit(solution)/shard_map/all_gather | solution.py:52
  159.6 11.5 %all_gather.32 = bf16[4,4,128,128]{3,2,1,0:T(8,128)(2,1)} all-gather(bf16[1,4,128,128]{3,2,1,0:T(8,128)(2,1)S(1)} %fusion.46), channel_id=1, replica_groups=mesh['seq_0'=4,'seq_1'=4,'seq_2'=2,'head'=4] {'seq_0'}, dimensions={0}, use_global_device_ids=true | all-gather | bytes 655360 | tf_op jit(solution)/shard_map/all_gather | solution.py:52
  171.1 6.6 %all-gather.3 = bf16[4,1,4]{2,1,0:T(2,128)(2,1)S(1)} all-gather(bf16[1,1,4]{2,1,0:T(2,128)(2,1)S(1)} %get-tuple-element.26), channel_id=1, replica_groups=mesh['seq_0'=4,'seq_1'=4,'seq_2'=2,'head'=4] {'seq_0'}, dimensions={0}, use_global_device_ids=true | all-gather | bytes 40 | tf_op jit(solution)/shard_map/all_gather | solution.py:52
  177.7 4.4 %fusion.3 = f32[512,4,128]{0,2,1:T(8,128)} fusion(f32[4,512]{1,0:T(4,128)S(1)} %bitcast.310, pred[512,512]{1,0:T(8,128)(4,1)} %iota_compare_fusion, bf16[512,1,4,128]{0,3,2,1:T(8,128)(2,1)} %copy.152, bf16[512,1,4,128]{3,2,1,0:T(4,128)(2,1)} %get-tuple-element.13, bf16[512,1,4,128]{3,2,1,0:T(4,128)(2,1)} %get-tuple-element.15), kind=kOutput, calls=%fused_computation.17 | convolution fusion | flops 542113792 | bytes 2891776 | tf_op jit(solution)/shard_map/hts,shd->thd/dot_general | solution.py:155
  182.1 3.4 %multiply_reduce_fusion.1 = (f32[512,4]{0,1:T(4,128)S(1)}, f32[512,4,128]{0,2,1:T(8,128)}) fusion(f32[512,4,128]{0,2,1:T(8,128)} %fusion.3, bf16[512,1,4,128]{3,2,1,0:T(4,128)(2,1)} %get-tuple-element.13, bf16[4,4,128,128]{3,2,1,0:T(8,128)(2,1)} %all_gather.32, f32[4]{0:T(128)S(1)} %get-tuple-element.33, f32[4]{0:T(128)S(1)} %get-tuple-element.31, ...), kind=kOutput, calls=%fused_computation.39 | convolution fusion | flops 70842368 | bytes 3948746 | tf_op jit(solution)/shard_map/thd,hde->the/dot_general | solution.py:167
  186.8 1.6 fusion.21
  191.2 4.4 %all-to-all-start.4 = ((bf16[4,512,512]{2,1,0:T(8,128)(2,1)}), bf16[4,512,512]{2,1,0:T(8,128)(2,1)}, u32[]{:S(2)}, u32[]{:S(2)}) async-start(bf16[4,512,512]{2,1,0:T(8,128)(2,1)} %bitcast.294), calls=%async_computation.4 | async-start | bytes 4194304 | tf_op jit(solution)/shard_map/all_to_all | solution.py:69
  195.7 16.7 %all-to-all-done.4 = bf16[4,512,512]{2,1,0:T(8,128)(2,1)} async-done(((bf16[4,512,512]{2,1,0:T(8,128)(2,1)}), bf16[4,512,512]{2,1,0:T(8,128)(2,1)}, u32[]{:S(2)}, u32[]{:S(2)}) %all-to-all-start.4) | async-done | bytes 2097184 | tf_op jit(solution)/shard_map/all_to_all | solution.py:69
  212.4 2.0 convert_reduce_fusion
  215.4 14.1 %all-to-all-start.5 = ((bf16[2,32,8,512]{3,2,0,1:T(8,128)(2,1)}), bf16[2,32,8,512]{3,2,0,1:T(8,128)(2,1)S(1)}, u32[]{:S(2)}, u32[]{:S(2)}) async-start(bf16[2,32,8,512]{3,2,0,1:T(8,128)(2,1)} %fusion.18), calls=%async_computation.5 | async-start | bytes 1048576 | tf_op jit(solution)/shard_map/all_to_all | solution.py:177
  229.9 11.3 %all-to-all-done.5 = bf16[2,32,8,512]{3,2,0,1:T(8,128)(2,1)S(1)} async-done(((bf16[2,32,8,512]{3,2,0,1:T(8,128)(2,1)}), bf16[2,32,8,512]{3,2,0,1:T(8,128)(2,1)S(1)}, u32[]{:S(2)}, u32[]{:S(2)}) %all-to-all-start.5) | async-done | bytes 524320 | tf_op jit(solution)/shard_map/all_to_all | solution.py:177
  242.0 15.0 %all_to_all.59 = bf16[32,2,8,512]{3,2,1,0:T(8,128)(2,1)S(1)} all-to-all(bf16[32,2,8,512]{3,2,1,0:T(8,128)(2,1)S(1)} %bitcast.301), channel_id=1, replica_groups=mesh['seq_0'=4,'seq_1'=4,'seq_2'=2,'head'=4] {'seq_0','seq_1','seq_2'}, dimensions={0} | all-to-all | bytes 1048576 | tf_op jit(solution)/shard_map/all_to_all | solution.py:184
  (82 shorter events, 19.5 us)
Async XLA Ops:
  0.6 187.8 %copy-start = (bf16[512,2048]{1,0:T(8,128)(2,1)S(1)}, bf16[512,2048]{1,0:T(8,128)(2,1)}, u32[]{:S(2)}) copy-start(bf16[512,2048]{1,0:T(8,128)(2,1)} %param.25) | copy-start | bytes 6291460
  4.2 5.0 %copy-start.7 = (s32[32]{0:T(128)S(1)}, s32[32]{0:T(128)}, u32[]{:S(2)}) copy-start(s32[32]{0:T(128)} %param.17) | copy-start | bytes 388
  4.2 30.9 %all-to-all-start = ((f32[4,256,512]{2,1,0:T(8,128)}), f32[4,256,512]{2,1,0:T(8,128)}, u32[]{:S(2)}, u32[]{:S(2)}) async-start(f32[4,256,512]{2,1,0:T(8,128)} %convolution_bitcast_fusion), calls=%async_computation | async-start | bytes 4194304 | tf_op jit(solution)/shard_map/all_to_all | solution.py:19
  9.1 27.8 %copy-start.2 = (bf16[256,512]{1,0:T(8,128)(2,1)S(1)}, bf16[256,512]{1,0:T(8,128)(2,1)}, u32[]{:S(2)}) copy-start(bf16[256,512]{1,0:T(8,128)(2,1)} %param.16) | copy-start | bytes 786436
  37.8 21.5 %all-to-all-start.1 = ((bf16[2,32,8,512]{3,2,0,1:T(8,128)(2,1)}), bf16[2,32,8,512]{3,2,0,1:T(8,128)(2,1)S(1)}, u32[]{:S(2)}, u32[]{:S(2)}) async-start(bf16[2,32,8,512]{3,2,0,1:T(8,128)(2,1)} %pad_maximum_fusion), calls=%async_computation.1 | async-start | bytes 1048576 | tf_op jit(solution)/shard_map/all_to_all | solution.py:116
  78.7 6.2 %copy-start.1 = (f32[32]{0:T(128)S(1)}, f32[32]{0:T(128)}, u32[]{:S(2)}) copy-start(f32[32]{0:T(128)} %param.18) | copy-start | bytes 388
  78.7 6.9 %copy-start.6 = (f32[4]{0:T(128)S(1)}, f32[4]{0:T(128)}, u32[]{:S(2)}) copy-start(f32[4]{0:T(128)} %param.23) | copy-start | bytes 52
  78.7 6.9 %copy-start.3 = (f32[2048]{0:T(1024)S(1)}, f32[2048]{0:T(1024)}, u32[]{:S(2)}) copy-start(f32[2048]{0:T(1024)} %param.20) | copy-start | bytes 24580
  78.7 31.4 %all-to-all-start.3 = ((bf16[4,512,512]{1,2,0:T(8,128)(2,1)}), bf16[4,512,512]{1,2,0:T(8,128)(2,1)}, u32[]{:S(2)}, u32[]{:S(2)}) async-start(bf16[4,512,512]{1,2,0:T(8,128)(2,1)} %broadcast_in_dim.53), calls=%async_computation.3 | async-start | bytes 4194304 | tf_op jit(solution)/shard_map/all_to_all | solution.py:31
  112.2 2.2 copy-start.4
  182.1 4.7 %copy-start.5 = (f32[4,128]{1,0:T(4,128)S(1)}, f32[4,128]{1,0:T(4,128)}, u32[]{:S(2)}) copy-start(f32[4,128]{1,0:T(4,128)} %param.24) | copy-start | bytes 6148
  191.2 21.2 %all-to-all-start.4 = ((bf16[4,512,512]{2,1,0:T(8,128)(2,1)}), bf16[4,512,512]{2,1,0:T(8,128)(2,1)}, u32[]{:S(2)}, u32[]{:S(2)}) async-start(bf16[4,512,512]{2,1,0:T(8,128)(2,1)} %bitcast.294), calls=%async_computation.4 | async-start | bytes 4194304 | tf_op jit(solution)/shard_map/all_to_all | solution.py:69
  215.4 25.8 %all-to-all-start.5 = ((bf16[2,32,8,512]{3,2,0,1:T(8,128)(2,1)}), bf16[2,32,8,512]{3,2,0,1:T(8,128)(2,1)S(1)}, u32[]{:S(2)}, u32[]{:S(2)}) async-start(bf16[2,32,8,512]{3,2,0,1:T(8,128)(2,1)} %fusion.18), calls=%async_computation.5 | async-start | bytes 1048576 | tf_op jit(solution)/shard_map/all_to_all | solution.py:177
where the time goes:
time: 259 us; the launch traced here: 258 us
  waiting for transfers between devices  78.7 us (30%)
  blocking collectives  68.5 us (26%)
  starting transfers between devices  38.2 us (15%)
  local copies, waits for them, and re-layouts  30.4 us (12%)
  matrix products  24 us (9%)
  other arithmetic  17.2 us (7%)
    all_gather x6, blocking collectives, entering_2(): lax.all_gather(part.astype(kind), axis)  38.5 us
    all_to_all x1, waiting for transfers between devices, sent_and_summed(): lax.all_to_all(pieces, axis, split_axis=0, concat_axis=0, tiled=True)  25.9 us
    all_to_all x1, waiting for transfers between devices, sent_and_summed_2(): lax.all_to_all(pieces, axis, split_axis=0, concat_axis=0, tiled=True)  16.7 us
    all_to_all x1, blocking collectives, shards(): lax.all_to_all(outgoing_units, SEQ, split_axis=0, concat_axis=2, tiled=True)  15 us
    all_to_all x1, blocking collectives, shards(): lax.all_to_all(outgoing, SEQ, split_axis=0, concat_axis=2, tiled=True)  15 us
    all_to_all x1, starting transfers between devices, shards(): lax.all_to_all(result_shares, SEQ, split_axis=1, concat_axis=1, tiled=True)  14.1 us
    all_to_all x1, waiting for transfers between devices, copy_for_each(): lax.all_to_all(jnp.broadcast_to(array[None], (length, *array.shape)), axi...  13.5 us
    unnamed x22, local copies, waits for them, and re-layouts  12.8 us
  transfers between devices with their start and end apart: 5, of which 5 were waited for; matrix products, arithmetic and copies ran while one was open for 5% of the time, Pallas kernels for 0%

commit v1 on v0

--- a/solution.py
+++ b/solution.py
@@ -113,7 +113,9 @@
     partial_value = jnp.dot(image_patches[0], adapter, preferred_element_type=jnp.float32)
     embedded = sent_and_summed(partial_value, "head", 1).astype(jnp.bfloat16)
     units_here = jnp.stack([embedded, text_embed]).reshape(2, seq_count, share_rows, local_width)
-    spread = lax.all_to_all(units_here, SEQ, split_axis=1, concat_axis=1, tiled=True)
+    parts = jnp.split(units_here, lax.axis_size(SEQ), axis=1)
+    incoming = lax.all_to_all(jnp.stack(parts), SEQ, 0, 0)
+    spread = jnp.concatenate(incoming, axis=1)
     table = spread.reshape(unit_count, share_rows, local_width)
     pick_index = is_text * seq_count + source
     outgoing_units = jnp.take(table, pick_index, axis=0).reshape(

time: 259 us -> 278 us (1.073)
  other arithmetic: 17.2 us -> 34.8 us
    unnamed x1 -> x32, other arithmetic: 0.07 us -> 18.7 us
where the time goes in v1:
time: 278 us; the launch traced here: 276 us
  waiting for transfers between devices  78.7 us (28%)
  blocking collectives  68.5 us (25%)
  starting transfers between devices  38.2 us (14%)
  other arithmetic  34.8 us (13%)
  local copies, waits for them, and re-layouts  31.2 us (11%)
  matrix products  23.9 us (9%)
    all_gather x6, blocking collectives, entering_2(): lax.all_gather(part.astype(kind), axis)  38.5 us
    all_to_all x1, waiting for transfers between devices, sent_and_summed(): lax.all_to_all(pieces, axis, split_axis=0, concat_axis=0, tiled=True)  25.9 us
    unnamed x32, other arithmetic  18.7 us
    all_to_all x1, waiting for transfers between devices, sent_and_summed_2(): lax.all_to_all(pieces, axis, split_axis=0, concat_axis=0, tiled=True)  16.7 us
    all_to_all x1, blocking collectives, shards(): lax.all_to_all(outgoing_units, SEQ, split_axis=0, concat_axis=2, tiled=True)  15 us
    all_to_all x1, blocking collectives, shards(): lax.all_to_all(outgoing, SEQ, split_axis=0, concat_axis=2, tiled=True)  15 us
    all_to_all x1, starting transfers between devices, shards(): lax.all_to_all(result_shares, SEQ, split_axis=1, concat_axis=1, tiled=True)  14.1 us
    all_to_all x1, waiting for transfers between devices, copy_for_each(): lax.all_to_all(jnp.broadcast_to(array[None], (length, *array.shape)), axi...  13.5 us
  transfers between devices with their start and end apart: 5, of which 5 were waited for; matrix products, arithmetic and copies ran while one was open for 5% of the time, Pallas kernels for 0%

profile of v1, /device:TPU:1, one launch (start us, length us, event | category | flops | bytes accessed | tf_op | source)
XLA Modules:
  0.0 276.3 jit_solution(5406481574580685936)
XLA Ops:
  0.6 3.5 %convolution_bitcast_fusion = f32[4,256,512]{2,1,0:T(8,128)} fusion(bf16[36,4,8,512]{3,2,1,0:T(8,128)(2,1)} %bitcast.436, bf16[1,256,288]{1,2,0:T(8,128)(2,1)} %param.15), kind=kOutput, calls=%fused_computation.77 | convolution fusion | flops 301989888 | bytes 3424256 | tf_op jit(solution)/shard_map/dot_general | solution.py:113
  4.2 5.0 %all-to-all-start = ((f32[4,256,512]{2,1,0:T(8,128)}), f32[4,256,512]{2,1,0:T(8,128)}, u32[]{:S(2)}, u32[]{:S(2)}) async-start(f32[4,256,512]{2,1,0:T(8,128)} %convolution_bitcast_fusion), calls=%async_computation | async-start | bytes 4194304 | tf_op jit(solution)/shard_map/all_to_all | solution.py:19
  9.2 25.9 %all-to-all-done = f32[4,256,512]{2,1,0:T(8,128)} async-done(((f32[4,256,512]{2,1,0:T(8,128)}), f32[4,256,512]{2,1,0:T(8,128)}, u32[]{:S(2)}, u32[]{:S(2)}) %all-to-all-start) | async-done | bytes 2097184 | tf_op jit(solution)/shard_map/all_to_all | solution.py:19
  35.1 1.8 reduce_sum.65
  56.2 9.9 %all-to-all-start.1 = ((bf16[32,2,1,8,512]{4,3,1,2,0:T(8,128)(2,1)}), bf16[32,2,1,8,512]{4,3,1,2,0:T(8,128)(2,1)S(1)}, u32[]{:S(2)}, u32[]{:S(2)}) async-start(bf16[32,2,1,8,512]{4,3,1,2,0:T(8,128)(2,1)} %constant_dynamic-update-slice_fusion), calls=%async_computation.1 | async-start | bytes 1048576 | tf_op jit(solution)/shard_map/all_to_all | solution.py:117
  66.4 11.2 %all-to-all-done.1 = bf16[32,2,1,8,512]{4,3,1,2,0:T(8,128)(2,1)S(1)} async-done(((bf16[32,2,1,8,512]{4,3,1,2,0:T(8,128)(2,1)}), bf16[32,2,1,8,512]{4,3,1,2,0:T(8,128)(2,1)S(1)}, u32[]{:S(2)}, u32[]{:S(2)}) %all-to-all-start.1) | async-done | bytes 524320 | tf_op jit(solution)/shard_map/all_to_all | solution.py:117
  78.5 15.0 %all_to_all.58 = bf16[32,2,8,512]{3,2,1,0:T(8,128)(2,1)S(1)} all-to-all(bf16[32,2,8,512]{3,2,1,0:T(8,128)(2,1)S(1)} %bitcast.431), channel_id=1, replica_groups=mesh['seq_0'=4,'seq_1'=4,'seq_2'=2,'head'=4] {'seq_0','seq_1','seq_2'}, dimensions={0} | all-to-all | bytes 1048576 | tf_op jit(solution)/shard_map/all_to_all | solution.py:124
  97.0 4.8 %all-to-all-start.3 = ((bf16[4,512,512]{1,2,0:T(8,128)(2,1)}), bf16[4,512,512]{1,2,0:T(8,128)(2,1)}, u32[]{:S(2)}, u32[]{:S(2)}) async-start(bf16[4,512,512]{1,2,0:T(8,128)(2,1)} %broadcast_in_dim.53), calls=%async_computation.3 | async-start | bytes 4194304 | tf_op jit(solution)/shard_map/all_to_all | solution.py:31
  104.0 10.2 %copy.231 = bf16[256,8,4,512]{3,1,2,0:T(8,128)(2,1)} copy(bf16[256,8,4,512]{3,2,1,0:T(4,128)(2,1)} %bitcast.425) | data formatting | bytes 16777216
  115.0 13.5 %all-to-all-done.3 = bf16[4,512,512]{1,2,0:T(8,128)(2,1)} async-done(((bf16[4,512,512]{1,2,0:T(8,128)(2,1)}), bf16[4,512,512]{1,2,0:T(8,128)(2,1)}, u32[]{:S(2)}, u32[]{:S(2)}) %all-to-all-start.3) | async-done | bytes 2097184 | tf_op jit(solution)/shard_map/all_to_all | solution.py:31
  128.4 2.1 multiply_reduce_fusion
  130.6 2.1 fusion.1
  135.2 2.2 multiply_convert_fusion
  137.4 9.1 %convolution_convert_fusion.1 = bf16[512,2048]{1,0:T(8,128)(2,1)} fusion(bf16[512,2048]{0,1:T(8,128)(2,1)S(1)} %bitcast.435, bf16[2048,2048]{1,0:T(8,128)(2,1)} %bitcast.426), kind=kOutput, calls=%fused_computation.13 | convolution fusion | flops 4296015872 | bytes 12582912 | tf_op jit(solution)/shard_map/dot_general | solution.py:131
  146.5 4.4 %reshape.369 = bf16[512,4,4,128]{3,2,1,0:T(4,128)(2,1)} reshape(bf16[512,2048]{1,0:T(8,128)(2,1)} %convolution_convert_fusion.1) | data formatting | bytes 4194304 | tf_op jit(solution)/shard_map/reshape | solution.py:134
  150.9 3.2 %fusion.160 = (bf16[512,1,4,128]{3,2,1,0:T(4,128)(2,1)}, bf16[512,1,4,128]{3,2,1,0:T(4,128)(2,1)}, bf16[512,1,4,128]{3,2,1,0:T(4,128)(2,1)S(1)}, bf16[512,1,4,128]{3,2,1,0:T(4,128)(2,1)}) fusion(bf16[512,4,4,128]{3,2,1,0:T(4,128)(2,1)} %reshape.369), kind=kLoop, calls=%fused_computation.366 | loop fusion | bytes 4194304 | tf_op jit(solution)/shard_map/slice | solution.py:147
  155.3 1.9 convolution_convert_fusion.2
  157.2 2.2 all-gather
  159.4 1.8 all-gather.1
  161.4 9.9 %all_gather.31 = bf16[4,4,128,128]{3,2,1,0:T(8,128)(2,1)S(1)} all-gather(bf16[1,4,128,128]{3,2,1,0:T(8,128)(2,1)S(1)} %fusion.52), channel_id=1, replica_groups=mesh['seq_0'=4,'seq_1'=4,'seq_2'=2,'head'=4] {'seq_1'}, dimensions={0}, use_global_device_ids=true | all-gather | bytes 655360 | tf_op jit(solution)/shard_map/all_gather | solution.py:52
  171.3 6.5 %all-gather.2 = bf16[4,1,4]{2,1,0:T(2,128)(2,1)S(1)} all-gather(bf16[1,1,4]{2,1,0:T(2,128)(2,1)S(1)} %get-tuple-element.32), channel_id=1, replica_groups=mesh['seq_0'=4,'seq_1'=4,'seq_2'=2,'head'=4] {'seq_1'}, dimensions={0}, use_global_device_ids=true | all-gather | bytes 40 | tf_op jit(solution)/shard_map/all_gather | solution.py:52
  177.9 11.5 %all_gather.32 = bf16[4,4,128,128]{3,2,1,0:T(8,128)(2,1)} all-gather(bf16[1,4,128,128]{3,2,1,0:T(8,128)(2,1)S(1)} %fusion.46), channel_id=1, replica_groups=mesh['seq_0'=4,'seq_1'=4,'seq_2'=2,'head'=4] {'seq_0'}, dimensions={0}, use_global_device_ids=true | all-gather | bytes 655360 | tf_op jit(solution)/shard_map/all_gather | solution.py:52
  189.5 6.6 %all-gather.3 = bf16[4,1,4]{2,1,0:T(2,128)(2,1)S(1)} all-gather(bf16[1,1,4]{2,1,0:T(2,128)(2,1)S(1)} %get-tuple-element.26), channel_id=1, replica_groups=mesh['seq_0'=4,'seq_1'=4,'seq_2'=2,'head'=4] {'seq_0'}, dimensions={0}, use_global_device_ids=true | all-gather | bytes 40 | tf_op jit(solution)/shard_map/all_gather | solution.py:52
  196.1 4.3 %fusion.3 = f32[512,4,128]{0,2,1:T(8,128)} fusion(f32[4,512]{1,0:T(4,128)S(1)} %bitcast.440, pred[512,512]{1,0:T(8,128)(4,1)} %iota_compare_fusion, bf16[512,1,4,128]{0,3,2,1:T(8,128)(2,1)} %copy.225, bf16[512,1,4,128]{3,2,1,0:T(4,128)(2,1)} %get-tuple-element.13, bf16[512,1,4,128]{3,2,1,0:T(4,128)(2,1)} %get-tuple-element.15), kind=kOutput, calls=%fused_computation.79 | convolution fusion | flops 542113792 | bytes 2891776 | tf_op jit(solution)/shard_map/hts,shd->thd/dot_general | solution.py:157
  200.4 3.4 %multiply_reduce_fusion.1 = (f32[512,4]{0,1:T(4,128)S(1)}, f32[512,4,128]{0,2,1:T(8,128)}) fusion(f32[512,4,128]{0,2,1:T(8,128)} %fusion.3, bf16[512,1,4,128]{3,2,1,0:T(4,128)(2,1)} %get-tuple-element.13, bf16[4,4,128,128]{3,2,1,0:T(8,128)(2,1)} %all_gather.32, f32[4]{0:T(128)S(1)} %get-tuple-element.33, f32[4]{0:T(128)S(1)} %get-tuple-element.31, ...), kind=kOutput, calls=%fused_computation.101 | convolution fusion | flops 70842368 | bytes 3948746 | tf_op jit(solution)/shard_map/thd,hde->the/dot_general | solution.py:169
  205.1 1.6 fusion.21
  209.6 4.4 %all-to-all-start.4 = ((bf16[4,512,512]{2,1,0:T(8,128)(2,1)}), bf16[4,512,512]{2,1,0:T(8,128)(2,1)}, u32[]{:S(2)}, u32[]{:S(2)}) async-start(bf16[4,512,512]{2,1,0:T(8,128)(2,1)} %bitcast.427), calls=%async_computation.4 | async-start | bytes 4194304 | tf_op jit(solution)/shard_map/all_to_all | solution.py:69
  214.0 16.7 %all-to-all-done.4 = bf16[4,512,512]{2,1,0:T(8,128)(2,1)} async-done(((bf16[4,512,512]{2,1,0:T(8,128)(2,1)}), bf16[4,512,512]{2,1,0:T(8,128)(2,1)}, u32[]{:S(2)}, u32[]{:S(2)}) %all-to-all-start.4) | async-done | bytes 2097184 | tf_op jit(solution)/shard_map/all_to_all | solution.py:69
  230.8 2.0 convert_reduce_fusion
  233.8 14.1 %all-to-all-start.5 = ((bf16[2,32,8,512]{3,2,0,1:T(8,128)(2,1)}), bf16[2,32,8,512]{3,2,0,1:T(8,128)(2,1)S(1)}, u32[]{:S(2)}, u32[]{:S(2)}) async-start(bf16[2,32,8,512]{3,2,0,1:T(8,128)(2,1)} %copy.219), calls=%async_computation.5 | async-start | bytes 1048576 | tf_op jit(solution)/shard_map/all_to_all | solution.py:179
  248.3 11.3 %all-to-all-done.5 = bf16[2,32,8,512]{3,2,0,1:T(8,128)(2,1)S(1)} async-done(((bf16[2,32,8,512]{3,2,0,1:T(8,128)(2,1)}), bf16[2,32,8,512]{3,2,0,1:T(8,128)(2,1)S(1)}, u32[]{:S(2)}, u32[]{:S(2)}) %all-to-all-start.5) | async-done | bytes 524320 | tf_op jit(solution)/shard_map/all_to_all | solution.py:179
  260.5 15.0 %all_to_all.59 = bf16[32,2,8,512]{3,2,1,0:T(8,128)(2,1)S(1)} all-to-all(bf16[32,2,8,512]{3,2,1,0:T(8,128)(2,1)S(1)} %bitcast.433), channel_id=1, replica_groups=mesh['seq_0'=4,'seq_1'=4,'seq_2'=2,'head'=4] {'seq_0','seq_1','seq_2'}, dimensions={0} | all-to-all | bytes 1048576 | tf_op jit(solution)/shard_map/all_to_all | solution.py:186
  (114 shorter events, 37.9 us)
Async XLA Ops:
  0.6 206.1 %copy-start = (bf16[512,2048]{1,0:T(8,128)(2,1)S(1)}, bf16[512,2048]{1,0:T(8,128)(2,1)}, u32[]{:S(2)}) copy-start(bf16[512,2048]{1,0:T(8,128)(2,1)} %param.25) | copy-start | bytes 6291460
  4.2 5.0 %copy-start.7 = (s32[32]{0:T(128)S(1)}, s32[32]{0:T(128)}, u32[]{:S(2)}) copy-start(s32[32]{0:T(128)} %param.17) | copy-start | bytes 388
  4.2 30.9 %all-to-all-start = ((f32[4,256,512]{2,1,0:T(8,128)}), f32[4,256,512]{2,1,0:T(8,128)}, u32[]{:S(2)}, u32[]{:S(2)}) async-start(f32[4,256,512]{2,1,0:T(8,128)} %convolution_bitcast_fusion), calls=%async_computation | async-start | bytes 4194304 | tf_op jit(solution)/shard_map/all_to_all | solution.py:19
  9.1 27.8 %copy-start.2 = (bf16[256,512]{1,0:T(8,128)(2,1)S(1)}, bf16[256,512]{1,0:T(8,128)(2,1)}, u32[]{:S(2)}) copy-start(bf16[256,512]{1,0:T(8,128)(2,1)} %param.16) | copy-start | bytes 786436
  56.2 21.5 %all-to-all-start.1 = ((bf16[32,2,1,8,512]{4,3,1,2,0:T(8,128)(2,1)}), bf16[32,2,1,8,512]{4,3,1,2,0:T(8,128)(2,1)S(1)}, u32[]{:S(2)}, u32[]{:S(2)}) async-start(bf16[32,2,1,8,512]{4,3,1,2,0:T(8,128)(2,1)} %constant_dynamic-update-slice_fusion), calls=%async_computation.1 | async-start | bytes 1048576 | tf_op jit(solution)/shard_map/all_to_all | solution.py:117
  97.0 6.2 %copy-start.1 = (f32[32]{0:T(128)S(1)}, f32[32]{0:T(128)}, u32[]{:S(2)}) copy-start(f32[32]{0:T(128)} %param.18) | copy-start | bytes 388
  97.0 6.9 %copy-start.6 = (f32[4]{0:T(128)S(1)}, f32[4]{0:T(128)}, u32[]{:S(2)}) copy-start(f32[4]{0:T(128)} %param.23) | copy-start | bytes 52
  97.0 6.9 %copy-start.3 = (f32[2048]{0:T(1024)S(1)}, f32[2048]{0:T(1024)}, u32[]{:S(2)}) copy-start(f32[2048]{0:T(1024)} %param.20) | copy-start | bytes 24580
  97.0 31.4 %all-to-all-start.3 = ((bf16[4,512,512]{1,2,0:T(8,128)(2,1)}), bf16[4,512,512]{1,2,0:T(8,128)(2,1)}, u32[]{:S(2)}, u32[]{:S(2)}) async-start(bf16[4,512,512]{1,2,0:T(8,128)(2,1)} %broadcast_in_dim.53), calls=%async_computation.3 | async-start | bytes 4194304 | tf_op jit(solution)/shard_map/all_to_all | solution.py:31
  130.6 2.2 copy-start.4
  200.4 4.7 %copy-start.5 = (f32[4,128]{1,0:T(4,128)S(1)}, f32[4,128]{1,0:T(4,128)}, u32[]{:S(2)}) copy-start(f32[4,128]{1,0:T(4,128)} %param.24) | copy-start | bytes 6148
  209.6 21.2 %all-to-all-start.4 = ((bf16[4,512,512]{2,1,0:T(8,128)(2,1)}), bf16[4,512,512]{2,1,0:T(8,128)(2,1)}, u32[]{:S(2)}, u32[]{:S(2)}) async-start(bf16[4,512,512]{2,1,0:T(8,128)(2,1)} %bitcast.427), calls=%async_computation.4 | async-start | bytes 4194304 | tf_op jit(solution)/shard_map/all_to_all | solution.py:69
  233.8 25.8 %all-to-all-start.5 = ((bf16[2,32,8,512]{3,2,0,1:T(8,128)(2,1)}), bf16[2,32,8,512]{3,2,0,1:T(8,128)(2,1)S(1)}, u32[]{:S(2)}, u32[]{:S(2)}) async-start(bf16[2,32,8,512]{3,2,0,1:T(8,128)(2,1)} %copy.219), calls=%async_computation.5 | async-start | bytes 1048576 | tf_op jit(solution)/shard_map/all_to_all | solution.py:179
